TPU v7x, 512 devices: a whole 4x8x8 slice. The times are simulated.
512 devices in a mesh: enc: 32 (over y, x), section: 8 (over z_lo, core), llmdp: 2 (over z_hi).
Axes of the slice: x: 4, y: 8, z: 8 (z_hi: 2, z_lo: 4; z = z_hi * 4 + z_lo), core: 2. Of those that a mesh axis runs over, the one named last changes fastest.
Arguments:
- patches: bfloat16 [8192, 3200], P('enc', ('section', 'llmdp')), may hold values from -6 to 6
- gain: float32 [3200], replicated, may hold values from 0.25 to 1.75
- shift: float32 [3200], replicated, may hold values from -3 to 3
- proj_weight: bfloat16 [3200, 8192], P('enc', ('section', 'llmdp')), may hold values from -0.109375 to 0.109375
- llm_rank: int32 [8192, 1], P('enc'), may hold values from 0 to 31; in each aligned block of 256 rows (0 to 255, 256 to 511, ...) at most 24 rows name the same one
- embed_grad: bfloat16 [24576, 8192], P('enc', ('section', 'llmdp')), may hold values from -0.59765625 to 0.59765625
Outputs:
- embeds_recv: bfloat16 [24576, 8192], P('enc', ('section', 'llmdp'))
- hidden_state_gradient: bfloat16 [8192, 3200], P('enc', ('section', 'llmdp'))
- grad_weight: float32 [3200, 8192], P('enc', ('section', 'llmdp'))
- gain_gradient: float32 [3200], P(('section', 'llmdp'))
- grad_shift: float32 [3200], P(('section', 'llmdp'))
Inputs may be any that keep to these rules, and one draw needn't show every extreme that they name: `llm_rank`: among the 256 rows of one device, at most 24 name the same owner, a bound that some block reaches.
All inputs are finite; a program needn't handle non-finite values.
Results may differ from a plain program's by a relative error of at most 0.018.
Values may be sent and summed in bfloat16 or wider, within the bound.
No kernel may reach another device: no remote copies, remote signals or barrier semaphores. Data moves between devices by JAX's collectives and lax.ppermute only.
A program may use at most 64 MiB of HBM per device.

v0:
```python
import jax
import jax.numpy as jnp
from jax import lax
from jax.sharding import Mesh
from jax.sharding import PartitionSpec as P

ENC = ("enc_0", "enc_1")
EPSILON = 1e-05


def whole_of(x, axes, dim):
    for axis in reversed(axes):
        x = lax.all_gather(x, axis, axis=dim, tiled=True)
    return x


def summed_rows(terms, axes):
    running = terms.astype(jnp.bfloat16)
    for axis in axes:
        running = lax.psum_scatter(running, axis, scatter_dimension=0, tiled=True)
    return running.astype(jnp.float32)


def copy_for_each(x, axis):
    peers = lax.axis_size(axis)
    return lax.all_to_all(jnp.broadcast_to(x[None], (peers, *x.shape)), axis, 0, 0, tiled=True)


def taken_together(x, axis):
    everything = copy_for_each(x, axis)
    return jnp.sum(everything, axis=0)


def packed_total(arrays, axis):
    ends = [0]
    for a in arrays:
        ends.append(ends[-1] + a.size)
    running = taken_together(jnp.concatenate([a.ravel() for a in arrays]), axis)
    return tuple((running[b:e].reshape(a.shape) for a, b, e in zip(arrays, ends, ends[1:])))


def body(patches, gain, shift, proj_weight, llm_rank, embed_grad):
    row_count = patches.shape[0]
    owned_width = patches.shape[1]
    width = gain.shape[0]
    out_cols = proj_weight.shape[1]
    column_start = lax.axis_index(("section", "llmdp")) * owned_width
    gain_own = lax.dynamic_slice_in_dim(gain, column_start, owned_width, 0)
    complete_rows = lax.all_gather(patches, ("section", "llmdp"), axis=1, tiled=True).astype(
        jnp.float32
    )
    row_average = jnp.mean(complete_rows, 1, keepdims=True)
    variance = jnp.mean(complete_rows * complete_rows, 1, keepdims=True) - row_average * row_average
    inverse_deviation = lax.rsqrt(variance + EPSILON)
    standardized_full = (complete_rows - row_average) * inverse_deviation
    normed_hidden = (standardized_full * gain + shift).astype(jnp.bfloat16)
    standardized_owned = lax.dynamic_slice_in_dim(standardized_full, column_start, owned_width, 1)
    weight_full = whole_of(proj_weight, ENC, 0)
    embed_acc = jnp.dot(normed_hidden, weight_full, preferred_element_type=jnp.float32)
    embed = embed_acc.astype(jnp.bfloat16)
    senders = lax.axis_size(ENC)
    most_slots = embed_grad.shape[0] // senders
    target = llm_rank[:, 0]
    owners = jnp.arange(senders, dtype=jnp.int32)
    hits = (target[:, None] == owners[None, :]).astype(jnp.int32)
    rank = jnp.sum((jnp.cumsum(hits, 0) - hits) * hits, 1)
    slot = target * most_slots + rank
    outgoing = jnp.zeros((senders * most_slots, out_cols), jnp.bfloat16).at[slot].set(embed)
    arrived = lax.all_to_all(
        outgoing.reshape(senders, most_slots, out_cols),
        ENC,
        split_axis=0,
        concat_axis=0,
        tiled=True,
    )
    embeds_recv = arrived.reshape(senders * most_slots, out_cols)
    returned = lax.all_to_all(
        embed_grad.reshape(senders, most_slots, out_cols),
        ENC,
        split_axis=0,
        concat_axis=0,
        tiled=True,
    )
    d_embed = returned.reshape(senders * most_slots, out_cols)[slot]
    partial_grad = lax.dot_general(
        d_embed, weight_full, (((1,), (1,)), ((), ())), preferred_element_type=jnp.float32
    )
    grad_weight = summed_rows(
        lax.dot_general(
            normed_hidden, d_embed, (((0,), (0,)), ((), ())), preferred_element_type=jnp.float32
        ),
        ENC,
    )
    group_count = width // owned_width
    pieces = partial_grad.astype(jnp.bfloat16).reshape(row_count, group_count, owned_width)
    columns = lax.all_to_all(pieces, ("section", "llmdp"), split_axis=1, concat_axis=1, tiled=True)
    owned_normalized_gradient = jnp.sum(columns.astype(jnp.float32), 1)
    owned_centered_gradient = owned_normalized_gradient * gain_own
    mean_sum, cross_sum = packed_total(
        (
            jnp.sum(owned_centered_gradient, 1),
            jnp.sum(owned_centered_gradient * standardized_owned, 1),
        ),
        ("section", "llmdp"),
    )
    gradient_row_average = (mean_sum / width)[:, None]
    gradient_cross_product = (cross_sum / width)[:, None]
    hidden_state_gradient = (
        inverse_deviation
        * (
            owned_centered_gradient
            - gradient_row_average
            - standardized_owned * gradient_cross_product
        )
    ).astype(jnp.bfloat16)
    gain_gradient, grad_shift = packed_total(
        (
            jnp.sum(owned_normalized_gradient * standardized_owned, 0),
            jnp.sum(owned_normalized_gradient, 0),
        ),
        ENC,
    )
    return (embeds_recv, hidden_state_gradient, grad_weight, gain_gradient, grad_shift)


def solution(mesh):
    split = Mesh(
        mesh.devices.reshape(8, 4, mesh.shape["section"], mesh.shape["llmdp"]),
        ("enc_0", "enc_1", "section", "llmdp"),
    )
    in_specs = (
        P(ENC, ("section", "llmdp")),
        P(),
        P(),
        P(ENC, ("section", "llmdp")),
        P(ENC, None),
        P(ENC, ("section", "llmdp")),
    )
    out_specs = (
        P(ENC, ("section", "llmdp")),
        P(ENC, ("section", "llmdp")),
        P(ENC, ("section", "llmdp")),
        P(("section", "llmdp")),
        P(("section", "llmdp")),
    )
    return jax.shard_map(body, mesh=split, in_specs=in_specs, out_specs=out_specs, check_vma=False)
```

profile of v0, /device:TPU:2, one launch (start us, length us, event | category | flops | bytes accessed | tf_op | source)
XLA Modules:
  0.0 333.3 jit_solution(10360011077139938337)
XLA Ops:
  7.2 0.0 all-gather.4.cloned.1.call-start
  7.2 0.7 all-gather.4.cloned.1.call-update
  7.9 0.0 all-gather.6.cloned.1.call-start
  8.0 15.6 %all-gather = bf16[4,100,512]{2,1,0:T(8,128)(2,1)S(1)} all-gather(bf16[1,100,512]{2,1,0:T(8,128)(2,1)} %bitcast.40), channel_id=1, replica_groups=mesh['enc_0'=8,'enc_1'=4,'section'=8,'llmdp'=2] {'enc_1'}, dimensions={0}, use_global_device_ids=true | all-gather | bytes 512000 | tf_op jit(solution)/shard_map/all_gather | solution.py:13
  23.5 0.8 reshape.100
  24.3 0.0 all-gather.6.cloned.1.call-update
  24.4 7.8 %all-to-all-start.1 = ((bf16[32,24,512]{2,1,0:T(8,128)(2,1)}), bf16[32,24,512]{2,1,0:T(8,128)(2,1)S(1)}, u32[]{:S(2)}, u32[]{:S(2)}) async-start(bf16[32,24,512]{2,1,0:T(8,128)(2,1)} %bitcast.39), calls=%async_computation.1 | async-start | bytes 1572864 | tf_op jit(solution)/shard_map/all_to_all | solution.py:77
  32.2 0.0 reduce-scatter.4.cloned.1.call-start
  32.2 0.6 reduce-window.6
  32.8 0.2 slice_reduce_fusion
  33.1 0.1 fusion.7
  33.2 18.2 %all-to-all-done.1 = bf16[32,24,512]{2,1,0:T(8,128)(2,1)S(1)} async-done(((bf16[32,24,512]{2,1,0:T(8,128)(2,1)}), bf16[32,24,512]{2,1,0:T(8,128)(2,1)S(1)}, u32[]{:S(2)}, u32[]{:S(2)}) %all-to-all-start.1) | async-done | bytes 786464 | tf_op jit(solution)/shard_map/all_to_all | solution.py:77
  51.4 1.2 gather_fusion
  52.6 80.3 %all-gather.4.cloned.1.call-done = bf16[256,3200]{0,1:T(8,128)(2,1)} async-done(((bf16[256,200]{0,1:T(8,128)(2,1)}), bf16[256,3200]{0,1:T(8,128)(2,1)}) %all-gather.4.cloned.1.call-update) | async-done | bytes 1638416 | tf_op jit(solution)/shard_map/all_gather | solution.py:49
  132.9 1.9 convert_reduce_fusion
  134.8 4.2 %convolution_convert_fusion = bf16[3200,512]{1,0:T(8,128)(2,1)} fusion(bf16[256,512]{1,0:T(8,128)(2,1)S(1)} %gather_fusion, f32[3200]{0:T(1024)S(1)} %copy-done.3, f32[3200]{0:T(1024)S(1)} %copy-done.2, f32[256]{0:T(256)S(1)} %get-tuple-element.17, f32[256]{0:T(256)S(1)} %get-tuple-element.16, bf16[256,3200]{0,1:T(8,128)(2,1)} %all-gather.4.cloned.1.call-done), kind=kOutput, calls=%fused_computation.2 | convolution fusion | flops 845414400 | bytes 5204992 | tf_op jit(solution)/shard_map/dot_general | solution.py:89
  139.0 0.0 reduce-scatter.4.cloned.1.call-update
  139.1 43.3 %all-gather.6.cloned.1.call-done = bf16[3200,512]{1,0:T(8,128)(2,1)} async-done(((bf16[400,512]{1,0:T(8,128)(2,1)}), bf16[3200,512]{1,0:T(8,128)(2,1)}) %all-gather.6.cloned.1.call-update) | async-done | bytes 3276816 | tf_op jit(solution)/shard_map/all_gather | solution.py:13
  182.3 4.1 %convolution_convert_fusion.2 = bf16[256,512]{1,0:T(8,128)(2,1)S(1)} fusion(bf16[3200,512]{1,0:T(8,128)(2,1)} %all-gather.6.cloned.1.call-done, f32[3200]{0:T(1024)S(1)} %copy-done.3, f32[3200]{0:T(1024)S(1)} %copy-done.2, f32[256]{0:T(256)S(1)} %get-tuple-element.17, f32[256]{0:T(256)S(1)} %get-tuple-element.16, bf16[256,3200]{0,1:T(8,128)(2,1)S(1)} %copy-done), kind=kOutput, calls=%fused_computation.12 | convolution fusion | flops 843907072 | bytes 5204992 | tf_op jit(solution)/shard_map/dot_general | solution.py:59
  186.4 2.5 scatter_custom_fusion
  188.9 7.6 %all-to-all-start = ((bf16[32,24,512]{2,1,0:T(8,128)(2,1)}), bf16[32,24,512]{2,1,0:T(8,128)(2,1)}, u32[]{:S(2)}, u32[]{:S(2)}) async-start(bf16[32,24,512]{2,1,0:T(8,128)(2,1)} %bitcast.6), calls=%async_computation | async-start | bytes 1572864 | tf_op jit(solution)/shard_map/all_to_all | solution.py:69
  196.5 3.0 convolution_convert_fusion.1
  199.5 2.2 copy.18
  201.8 25.3 %all-to-all-done = bf16[32,24,512]{2,1,0:T(8,128)(2,1)} async-done(((bf16[32,24,512]{2,1,0:T(8,128)(2,1)}), bf16[32,24,512]{2,1,0:T(8,128)(2,1)}, u32[]{:S(2)}, u32[]{:S(2)}) %all-to-all-start) | async-done | bytes 786464 | tf_op jit(solution)/shard_map/all_to_all | solution.py:69
  227.1 7.5 %all-to-all-start.2 = ((bf16[256,16,200]{0,2,1:T(8,128)(2,1)}), bf16[256,16,200]{0,2,1:T(8,128)(2,1)S(1)}, u32[]{:S(2)}, u32[]{:S(2)}) async-start(bf16[256,16,200]{0,2,1:T(8,128)(2,1)} %bitcast.38), calls=%async_computation.2 | async-start | bytes 3276800 | tf_op jit(solution)/shard_map/all_to_all | solution.py:96
  234.6 0.8 dynamic_slice.6
  235.4 1.3 dynamic-slice.4
  237.3 2.0 fusion.1
  239.4 36.7 %all-to-all-done.2 = bf16[256,16,200]{0,2,1:T(8,128)(2,1)S(1)} async-done(((bf16[256,16,200]{0,2,1:T(8,128)(2,1)}), bf16[256,16,200]{0,2,1:T(8,128)(2,1)S(1)}, u32[]{:S(2)}, u32[]{:S(2)}) %all-to-all-start.2) | async-done | bytes 1638432 | tf_op jit(solution)/shard_map/all_to_all | solution.py:96
  276.1 0.4 convert_reduce_fusion.1
  276.5 1.1 multiply_reduce_fusion
  277.6 0.6 broadcast_in_dim.7
  278.2 3.5 %all-to-all-start.3 = ((f32[16,1,512]{2,1,0:T(1,128)}), f32[16,1,512]{2,1,0:T(1,128)S(1)}, u32[]{:S(2)}, u32[]{:S(2)}) async-start(f32[16,1,512]{2,1,0:T(1,128)} %broadcast_in_dim.7), calls=%async_computation.3 | async-start | bytes 65536 | tf_op jit(solution)/shard_map/all_to_all | solution.py:26
  281.7 0.1 pad_maximum_fusion.1
  281.8 7.6 %all-to-all-done.3 = f32[16,1,512]{2,1,0:T(1,128)S(1)} async-done(((f32[16,1,512]{2,1,0:T(1,128)}), f32[16,1,512]{2,1,0:T(1,128)S(1)}, u32[]{:S(2)}, u32[]{:S(2)}) %all-to-all-start.3) | async-done | bytes 32800 | tf_op jit(solution)/shard_map/all_to_all | solution.py:26
  289.4 0.7 broadcast_in_dim.8
  290.1 5.3 %all-to-all-start.4 = ((f32[32,1,400]{2,1,0:T(1,128)}), f32[32,1,400]{2,1,0:T(1,128)S(1)}, u32[]{:S(2)}, u32[]{:S(2)}) async-start(f32[32,1,400]{2,1,0:T(1,128)} %broadcast_in_dim.8), calls=%async_computation.5 | async-start | bytes 131072 | tf_op jit(solution)/shard_map/all_to_all | solution.py:26
  295.4 1.7 multiply_convert_fusion
  297.1 7.0 %all-to-all-done.4 = f32[32,1,400]{2,1,0:T(1,128)S(1)} async-done(((f32[32,1,400]{2,1,0:T(1,128)}), f32[32,1,400]{2,1,0:T(1,128)S(1)}, u32[]{:S(2)}, u32[]{:S(2)}) %all-to-all-start.4) | async-done | bytes 51232 | tf_op jit(solution)/shard_map/all_to_all | solution.py:26
  304.0 0.1 reduce_sum.102
  304.1 0.0 reduce-scatter.4.cloned.1.call-done
  304.1 14.1 %fusion = bf16[104,512]{1,0:T(8,128)(2,1)S(1)} fusion(bf16[400,512]{1,0:T(8,128)(2,1)} %reduce-scatter.4.cloned.1.call-done), kind=kCustom, calls=%all-reduce-scatter | all-reduce-scatter fusion | flops 212993 | bytes 518144
  318.2 2.6 collective-permute-start
  320.8 0.6 fusion.9
  321.4 2.4 collective-permute-done
  323.8 0.2 concatenate.8
  324.0 0.7 dynamic-slice_convert_fusion
  324.7 2.1 copy.30
  (18 shorter events, 0.2 us)
Async XLA Ops:
  7.2 25.1 %copy-start.1 = (s32[256,1]{0,1:T(1,128)S(1)}, s32[256,1]{0,1:T(1,128)}, u32[]{:S(2)}) copy-start(s32[256,1]{0,1:T(1,128)} %param.10) | copy-start | bytes 3076
  7.2 125.7 %all-gather.4.cloned.1.call-start = ((), (), s32[]{:S(2)}) async-start(), calls=%async_computation.6 | async-start | bytes 1740800 | tf_op jit(solution)/shard_map/all_gather | solution.py:49
  7.9 174.4 %all-gather.6.cloned.1.call-start = ((), (), s32[]{:S(2)}) async-start(), calls=%async_computation.7 | async-start | bytes 3686400 | tf_op jit(solution)/shard_map/all_gather | solution.py:13
  24.3 110.5 %copy-start.2 = (f32[3200]{0:T(1024)S(1)}, f32[3200]{0:T(1024)}, u32[]{:S(2)}) copy-start(f32[3200]{0:T(1024)} %param.7) | copy-start | bytes 38404
  24.3 110.5 %copy-start.3 = (f32[3200]{0:T(1024)S(1)}, f32[3200]{0:T(1024)}, u32[]{:S(2)}) copy-start(f32[3200]{0:T(1024)} %param.8) | copy-start | bytes 38404
  24.4 27.1 %all-to-all-start.1 = ((bf16[32,24,512]{2,1,0:T(8,128)(2,1)}), bf16[32,24,512]{2,1,0:T(8,128)(2,1)S(1)}, u32[]{:S(2)}, u32[]{:S(2)}) async-start(bf16[32,24,512]{2,1,0:T(8,128)(2,1)} %bitcast.39), calls=%async_computation.1 | async-start | bytes 1572864 | tf_op jit(solution)/shard_map/all_to_all | solution.py:77
  32.2 271.9 %reduce-scatter.4.cloned.1.call-start = ((), (), s32[]{:S(2)}) async-start(), calls=%async_computation.8 | async-start | bytes 3686400 | tf_op jit(solution)/shard_map/reduce_scatter | solution.py:20
  139.0 43.3 %copy-start = (bf16[256,3200]{0,1:T(8,128)(2,1)S(1)}, bf16[256,3200]{0,1:T(8,128)(2,1)}, u32[]{:S(2)}) copy-start(bf16[256,3200]{0,1:T(8,128)(2,1)} %all-gather.4.cloned.1.call-done) | copy-start | bytes 4915204
  188.9 38.3 %all-to-all-start = ((bf16[32,24,512]{2,1,0:T(8,128)(2,1)}), bf16[32,24,512]{2,1,0:T(8,128)(2,1)}, u32[]{:S(2)}, u32[]{:S(2)}) async-start(bf16[32,24,512]{2,1,0:T(8,128)(2,1)} %bitcast.6), calls=%async_computation | async-start | bytes 1572864 | tf_op jit(solution)/shard_map/all_to_all | solution.py:69
  227.1 49.0 %all-to-all-start.2 = ((bf16[256,16,200]{0,2,1:T(8,128)(2,1)}), bf16[256,16,200]{0,2,1:T(8,128)(2,1)S(1)}, u32[]{:S(2)}, u32[]{:S(2)}) async-start(bf16[256,16,200]{0,2,1:T(8,128)(2,1)} %bitcast.38), calls=%async_computation.2 | async-start | bytes 3276800 | tf_op jit(solution)/shard_map/all_to_all | solution.py:96
  278.2 11.2 %all-to-all-start.3 = ((f32[16,1,512]{2,1,0:T(1,128)}), f32[16,1,512]{2,1,0:T(1,128)S(1)}, u32[]{:S(2)}, u32[]{:S(2)}) async-start(f32[16,1,512]{2,1,0:T(1,128)} %broadcast_in_dim.7), calls=%async_computation.3 | async-start | bytes 65536 | tf_op jit(solution)/shard_map/all_to_all | solution.py:26
  290.1 14.0 %all-to-all-start.4 = ((f32[32,1,400]{2,1,0:T(1,128)}), f32[32,1,400]{2,1,0:T(1,128)S(1)}, u32[]{:S(2)}, u32[]{:S(2)}) async-start(f32[32,1,400]{2,1,0:T(1,128)} %broadcast_in_dim.8), calls=%async_computation.5 | async-start | bytes 131072 | tf_op jit(solution)/shard_map/all_to_all | solution.py:26
  318.2 5.6 %collective-permute-start = (bf16[12,512]{1,0:T(8,128)(2,1)S(1)}, bf16[12,512]{1,0:T(8,128)(2,1)S(1)}, u32[]{:S(2)}, u32[]{:S(2)}) collective-permute-start(bf16[12,512]{1,0:T(8,128)(2,1)S(1)} %slice.27), channel_id=1, source_target_pairs={{0,16},{16,32},{32,48},{1,17},{17,33},{33,49},{2,18},{18,34},{34,5... | collective-permute-start | bytes 36872
Sparse Core Ops, SparseCore 0:
  10.1 122.7 all-gather.3
  135.6 46.7 all-gather.5
  185.2 62.8 reduce-scatter.3
where the time goes:
time: 334 us; the launch traced here: 333 us
  waiting for transfers between devices  222 us (66%)
  starting transfers between devices  34.4 us (10%)
  blocking collectives  29.6 us (9%)
  between operations  14.6 us (4%)
  local copies, waits for them, and re-layouts  13.1 us (4%)
  matrix products  11.3 us (3%)
  other arithmetic  8.74 us (3%)
    all_gather x1, waiting for transfers between devices, body(): lax.all_gather(patches, ('section', 'llmdp'), axis=1, tiled=True)  80.3 us
    all_gather x1, waiting for transfers between devices, whole_of(): x = lax.all_gather(x, axis, axis=dim, tiled=True)  43.3 us
    all_to_all x1, waiting for transfers between devices, body(): lax.all_to_all(pieces, ('section', 'llmdp'), split_axis=1, concat_axis=1,...  36.7 us
    all_to_all x1, waiting for transfers between devices, body(): lax.all_to_all(outgoing.reshape(senders, most_slots, out_cols), ENC, spli...  25.3 us
    all_to_all x1, waiting for transfers between devices, body(): lax.all_to_all(embed_grad.reshape(senders, most_slots, out_cols), ENC, sp...  18.2 us
    all_gather x1, blocking collectives, whole_of(): x = lax.all_gather(x, axis, axis=dim, tiled=True)  15.6 us
    all_to_all x2, waiting for transfers between devices, copy_for_each(): lax.all_to_all(jnp.broadcast_to(x[None], (peers, *x.shape)), axis, 0, 0,...  14.6 us
    unnamed x1, blocking collectives  14.1 us
  transfers between devices with their start and end apart: 9, of which 8 were waited for; matrix products, arithmetic and copies ran while one was open for 9% of the time, Pallas kernels for 0%

commit v1 on v0

--- a/solution.py
+++ b/solution.py
@@ -93,7 +93,9 @@
     )
     group_count = width // owned_width
     pieces = partial_grad.astype(jnp.bfloat16).reshape(row_count, group_count, owned_width)
-    columns = lax.all_to_all(pieces, ("section", "llmdp"), split_axis=1, concat_axis=1, tiled=True)
+    cells = jnp.split(pieces, lax.axis_size(("section", "llmdp")), axis=1)
+    incoming = lax.all_to_all(jnp.stack(cells), ("section", "llmdp"), 0, 0)
+    columns = jnp.concatenate(incoming, axis=1)
     owned_normalized_gradient = jnp.sum(columns.astype(jnp.float32), 1)
     owned_centered_gradient = owned_normalized_gradient * gain_own
     mean_sum, cross_sum = packed_total(

time: 334 us -> 333 us (level)
  waiting for transfers between devices: 222 us -> 212 us
  local copies, waits for them, and re-layouts: 13.1 us -> 21.7 us
    all_to_all x1, waiting for transfers between devices: 25.3 us -> 16.6 us  [body(): lax.all_to_all(outgoing.reshape(senders, most_slots, out_cols), ENC, spli...]
    unnamed x13 -> x32, local copies, waits for them, and re-layouts: 4.35 us -> 12.9 us
    all_gather x1, waiting for transfers between devices: 80.3 us -> 73.3 us  [body(): lax.all_gather(patches, ('section', 'llmdp'), axis=1, tiled=True)]
    all_gather x1, waiting for transfers between devices: 43.3 us -> 49.5 us  [whole_of(): x = lax.all_gather(x, axis, axis=dim, tiled=True)]
  transfers between devices with their start and end apart: 9 -> 9, of which waited for: 8 -> 8; matrix products, arithmetic and copies ran while one was open for 9% -> 11% of each run, Pallas kernels for 0% -> 0%
where the time goes in v1:
time: 333 us; the launch traced here: 332 us
  waiting for transfers between devices  212 us (64%)
  starting transfers between devices  34.4 us (10%)
  blocking collectives  29.6 us (9%)
  local copies, waits for them, and re-layouts  21.7 us (7%)
  between operations  14.7 us (4%)
  matrix products  10.3 us (3%)
  other arithmetic  8.86 us (3%)
    all_gather x1, waiting for transfers between devices, body(): lax.all_gather(patches, ('section', 'llmdp'), axis=1, tiled=True)  73.3 us
    all_gather x1, waiting for transfers between devices, whole_of(): x = lax.all_gather(x, axis, axis=dim, tiled=True)  49.5 us
    all_to_all x1, waiting for transfers between devices, body(): incoming = lax.all_to_all(jnp.stack(cells), ('section', 'llmdp'), 0, 0)  36.7 us
    all_to_all x1, waiting for transfers between devices, body(): lax.all_to_all(embed_grad.reshape(senders, most_slots, out_cols), ENC, sp...  18.2 us
    all_to_all x1, waiting for transfers between devices, body(): lax.all_to_all(outgoing.reshape(senders, most_slots, out_cols), ENC, spli...  16.6 us
    all_gather x1, blocking collectives, whole_of(): x = lax.all_gather(x, axis, axis=dim, tiled=True)  15.6 us
    all_to_all x2, waiting for transfers between devices, copy_for_each(): lax.all_to_all(jnp.broadcast_to(x[None], (peers, *x.shape)), axis, 0, 0,...  14.6 us
    unnamed x1, blocking collectives  14.1 us
  transfers between devices with their start and end apart: 9, of which 8 were waited for; matrix products, arithmetic and copies ran while one was open for 11% of the time, Pallas kernels for 0%

profile of v1, /device:TPU:2, one launch (start us, length us, event | category | flops | bytes accessed | tf_op | source)
XLA Modules:
  0.0 331.6 jit_solution(7865586624540790409)
XLA Ops:
  7.2 0.7 all-gather.4.cloned.1.call-update
  8.0 15.6 %all-gather = bf16[4,100,512]{2,1,0:T(8,128)(2,1)S(1)} all-gather(bf16[1,100,512]{2,1,0:T(8,128)(2,1)} %bitcast.117), channel_id=1, replica_groups=mesh['enc_0'=8,'enc_1'=4,'section'=8,'llmdp'=2] {'enc_1'}, dimensions={0}, use_global_device_ids=true | all-gather | bytes 512000 | tf_op jit(solution)/shard_map/all_gather | solution.py:13
  23.5 0.8 reshape.103
  24.4 7.8 %all-to-all-start.1 = ((bf16[32,24,512]{2,1,0:T(8,128)(2,1)}), bf16[32,24,512]{2,1,0:T(8,128)(2,1)S(1)}, u32[]{:S(2)}, u32[]{:S(2)}) async-start(bf16[32,24,512]{2,1,0:T(8,128)(2,1)} %bitcast.8), calls=%async_computation.1 | async-start | bytes 1572864 | tf_op jit(solution)/shard_map/all_to_all | solution.py:77
  32.2 0.6 reduce-window.6
  32.8 0.2 slice_reduce_fusion
  33.2 18.2 %all-to-all-done.1 = bf16[32,24,512]{2,1,0:T(8,128)(2,1)S(1)} async-done(((bf16[32,24,512]{2,1,0:T(8,128)(2,1)}), bf16[32,24,512]{2,1,0:T(8,128)(2,1)S(1)}, u32[]{:S(2)}, u32[]{:S(2)}) %all-to-all-start.1) | async-done | bytes 786464 | tf_op jit(solution)/shard_map/all_to_all | solution.py:77
  51.4 1.2 gather_fusion
  52.6 73.3 %all-gather.4.cloned.1.call-done = bf16[256,3200]{0,1:T(8,128)(2,1)} async-done(((bf16[256,200]{0,1:T(8,128)(2,1)}), bf16[256,3200]{0,1:T(8,128)(2,1)}) %all-gather.4.cloned.1.call-update) | async-done | bytes 1638416 | tf_op jit(solution)/shard_map/all_gather | solution.py:49
  125.9 2.0 convert_reduce_fusion
  128.0 3.2 convolution_convert_fusion
  131.2 49.5 %all-gather.6.cloned.1.call-done = bf16[3200,512]{1,0:T(8,128)(2,1)} async-done(((bf16[400,512]{1,0:T(8,128)(2,1)}), bf16[3200,512]{1,0:T(8,128)(2,1)}) %all-gather.6.cloned.1.call-update) | async-done | bytes 3276816 | tf_op jit(solution)/shard_map/all_gather | solution.py:13
  180.7 4.1 %convolution_convert_fusion.2 = bf16[256,512]{1,0:T(8,128)(2,1)S(1)} fusion(bf16[3200,512]{1,0:T(8,128)(2,1)} %all-gather.6.cloned.1.call-done, f32[3200]{0:T(1024)S(1)} %copy-done.5, f32[3200]{0:T(1024)S(1)} %copy-done.4, f32[256]{0:T(256)S(1)} %get-tuple-element.17, f32[256]{0:T(256)S(1)} %get-tuple-element.16, bf16[256,3200]{0,1:T(8,128)(2,1)S(1)} %copy-done), kind=kOutput, calls=%fused_computation.12 | convolution fusion | flops 843907072 | bytes 5204992 | tf_op jit(solution)/shard_map/dot_general | solution.py:59
  184.7 2.5 scatter_custom_fusion
  187.2 7.6 %all-to-all-start = ((bf16[32,24,512]{2,1,0:T(8,128)(2,1)}), bf16[32,24,512]{2,1,0:T(8,128)(2,1)}, u32[]{:S(2)}, u32[]{:S(2)}) async-start(bf16[32,24,512]{2,1,0:T(8,128)(2,1)} %bitcast.6), calls=%async_computation | async-start | bytes 1572864 | tf_op jit(solution)/shard_map/all_to_all | solution.py:69
  194.9 3.1 convolution_convert_fusion.1
  197.9 2.3 copy.33
  200.2 1.0 fusion.20
  201.2 0.9 fusion.19
  202.1 0.9 fusion.18
  203.0 0.9 fusion.17
  203.9 0.9 fusion.16
  204.8 0.9 fusion.15
  205.7 0.9 fusion.14
  206.6 0.9 fusion.13
  207.7 1.2 copy-done.2
  208.9 16.6 %all-to-all-done = bf16[32,24,512]{2,1,0:T(8,128)(2,1)} async-done(((bf16[32,24,512]{2,1,0:T(8,128)(2,1)}), bf16[32,24,512]{2,1,0:T(8,128)(2,1)}, u32[]{:S(2)}, u32[]{:S(2)}) %all-to-all-start) | async-done | bytes 786464 | tf_op jit(solution)/shard_map/all_to_all | solution.py:69
  225.5 7.5 %all-to-all-start.2 = ((bf16[16,256,1,200]{1,3,2,0:T(8,128)(2,1)}), bf16[16,256,1,200]{1,3,2,0:T(8,128)(2,1)S(1)}, u32[]{:S(2)}, u32[]{:S(2)}) async-start(bf16[16,256,1,200]{1,3,2,0:T(8,128)(2,1)} %copy-done.2), calls=%async_computation.2 | async-start | bytes 3276800 | tf_op jit(solution)/shard_map/all_to_all | solution.py:97
  233.0 0.8 dynamic_slice.6
  233.8 1.3 dynamic-slice.4
  235.7 2.0 fusion.1
  237.7 36.7 %all-to-all-done.2 = bf16[16,256,1,200]{1,3,2,0:T(8,128)(2,1)S(1)} async-done(((bf16[16,256,1,200]{1,3,2,0:T(8,128)(2,1)}), bf16[16,256,1,200]{1,3,2,0:T(8,128)(2,1)S(1)}, u32[]{:S(2)}, u32[]{:S(2)}) %all-to-all-start.2) | async-done | bytes 1638432 | tf_op jit(solution)/shard_map/all_to_all | solution.py:97
  274.4 0.4 convert_reduce_fusion.1
  274.8 1.1 multiply_reduce_fusion
  275.9 0.6 broadcast_in_dim.7
  276.5 3.5 %all-to-all-start.3 = ((f32[16,1,512]{2,1,0:T(1,128)}), f32[16,1,512]{2,1,0:T(1,128)S(1)}, u32[]{:S(2)}, u32[]{:S(2)}) async-start(f32[16,1,512]{2,1,0:T(1,128)} %broadcast_in_dim.7), calls=%async_computation.3 | async-start | bytes 65536 | tf_op jit(solution)/shard_map/all_to_all | solution.py:26
  280.1 7.6 %all-to-all-done.3 = f32[16,1,512]{2,1,0:T(1,128)S(1)} async-done(((f32[16,1,512]{2,1,0:T(1,128)}), f32[16,1,512]{2,1,0:T(1,128)S(1)}, u32[]{:S(2)}, u32[]{:S(2)}) %all-to-all-start.3) | async-done | bytes 32800 | tf_op jit(solution)/shard_map/all_to_all | solution.py:26
  287.7 0.7 broadcast_in_dim.8
  288.4 5.2 %all-to-all-start.4 = ((f32[32,1,400]{2,1,0:T(1,128)}), f32[32,1,400]{2,1,0:T(1,128)S(1)}, u32[]{:S(2)}, u32[]{:S(2)}) async-start(f32[32,1,400]{2,1,0:T(1,128)} %broadcast_in_dim.8), calls=%async_computation.5 | async-start | bytes 131072 | tf_op jit(solution)/shard_map/all_to_all | solution.py:26
  293.7 1.7 multiply_convert_fusion
  295.4 7.0 %all-to-all-done.4 = f32[32,1,400]{2,1,0:T(1,128)S(1)} async-done(((f32[32,1,400]{2,1,0:T(1,128)}), f32[32,1,400]{2,1,0:T(1,128)S(1)}, u32[]{:S(2)}, u32[]{:S(2)}) %all-to-all-start.4) | async-done | bytes 51232 | tf_op jit(solution)/shard_map/all_to_all | solution.py:26
  302.4 14.1 %fusion = bf16[104,512]{1,0:T(8,128)(2,1)S(1)} fusion(bf16[400,512]{1,0:T(8,128)(2,1)} %reduce-scatter.4.cloned.1.call-done), kind=kCustom, calls=%all-reduce-scatter | all-reduce-scatter fusion | flops 212993 | bytes 518144
  316.5 2.6 collective-permute-start
  319.1 0.6 fusion.25
  319.8 2.4 collective-permute-done
  322.1 0.2 concatenate.8
  322.3 0.7 dynamic-slice_convert_fusion
  323.0 2.1 copy.60
  (38 shorter events, 0.6 us)
Async XLA Ops:
  7.2 118.8 %all-gather.4.cloned.1.call-start = ((), (), s32[]{:S(2)}) async-start(), calls=%async_computation.6 | async-start | bytes 1740800 | tf_op jit(solution)/shard_map/all_gather | solution.py:49
  7.9 172.8 %all-gather.6.cloned.1.call-start = ((), (), s32[]{:S(2)}) async-start(), calls=%async_computation.7 | async-start | bytes 3686400 | tf_op jit(solution)/shard_map/all_gather | solution.py:13
  7.9 24.3 %copy-start.3 = (s32[256,1]{0,1:T(1,128)S(1)}, s32[256,1]{0,1:T(1,128)}, u32[]{:S(2)}) copy-start(s32[256,1]{0,1:T(1,128)} %param.10) | copy-start | bytes 3076
  24.4 27.1 %all-to-all-start.1 = ((bf16[32,24,512]{2,1,0:T(8,128)(2,1)}), bf16[32,24,512]{2,1,0:T(8,128)(2,1)S(1)}, u32[]{:S(2)}, u32[]{:S(2)}) async-start(bf16[32,24,512]{2,1,0:T(8,128)(2,1)} %bitcast.8), calls=%async_computation.1 | async-start | bytes 1572864 | tf_op jit(solution)/shard_map/all_to_all | solution.py:77
  32.2 270.3 %reduce-scatter.4.cloned.1.call-start = ((), (), s32[]{:S(2)}) async-start(), calls=%async_computation.8 | async-start | bytes 3686400 | tf_op jit(solution)/shard_map/reduce_scatter | solution.py:20
  51.4 76.5 %copy-start.4 = (f32[3200]{0:T(1024)S(1)}, f32[3200]{0:T(1024)}, u32[]{:S(2)}) copy-start(f32[3200]{0:T(1024)} %param.7) | copy-start | bytes 38404
  51.4 76.5 %copy-start.5 = (f32[3200]{0:T(1024)S(1)}, f32[3200]{0:T(1024)}, u32[]{:S(2)}) copy-start(f32[3200]{0:T(1024)} %param.8) | copy-start | bytes 38404
  125.9 2.1 copy-start
  187.2 38.3 %all-to-all-start = ((bf16[32,24,512]{2,1,0:T(8,128)(2,1)}), bf16[32,24,512]{2,1,0:T(8,128)(2,1)}, u32[]{:S(2)}, u32[]{:S(2)}) async-start(bf16[32,24,512]{2,1,0:T(8,128)(2,1)} %bitcast.6), calls=%async_computation | async-start | bytes 1572864 | tf_op jit(solution)/shard_map/all_to_all | solution.py:69
  200.2 7.3 %copy-start.1 = (bf16[256,3200]{0,1:T(8,128)(2,1)S(1)}, bf16[256,3200]{0,1:T(8,128)(2,1)}, u32[]{:S(2)}) copy-start(bf16[256,3200]{0,1:T(8,128)(2,1)} %copy.33) | copy-start | bytes 4915204
  207.7 1.2 copy-start.2
  225.5 49.0 %all-to-all-start.2 = ((bf16[16,256,1,200]{1,3,2,0:T(8,128)(2,1)}), bf16[16,256,1,200]{1,3,2,0:T(8,128)(2,1)S(1)}, u32[]{:S(2)}, u32[]{:S(2)}) async-start(bf16[16,256,1,200]{1,3,2,0:T(8,128)(2,1)} %copy-done.2), calls=%async_computation.2 | async-start | bytes 3276800 | tf_op jit(solution)/shard_map/all_to_all | solution.py:97
  276.5 11.2 %all-to-all-start.3 = ((f32[16,1,512]{2,1,0:T(1,128)}), f32[16,1,512]{2,1,0:T(1,128)S(1)}, u32[]{:S(2)}, u32[]{:S(2)}) async-start(f32[16,1,512]{2,1,0:T(1,128)} %broadcast_in_dim.7), calls=%async_computation.3 | async-start | bytes 65536 | tf_op jit(solution)/shard_map/all_to_all | solution.py:26
  288.4 13.9 %all-to-all-start.4 = ((f32[32,1,400]{2,1,0:T(1,128)}), f32[32,1,400]{2,1,0:T(1,128)S(1)}, u32[]{:S(2)}, u32[]{:S(2)}) async-start(f32[32,1,400]{2,1,0:T(1,128)} %broadcast_in_dim.8), calls=%async_computation.5 | async-start | bytes 131072 | tf_op jit(solution)/shard_map/all_to_all | solution.py:26
  316.5 5.6 %collective-permute-start = (bf16[12,512]{1,0:T(8,128)(2,1)S(1)}, bf16[12,512]{1,0:T(8,128)(2,1)S(1)}, u32[]{:S(2)}, u32[]{:S(2)}) collective-permute-start(bf16[12,512]{1,0:T(8,128)(2,1)S(1)} %slice.27), channel_id=1, source_target_pairs={{0,16},{16,32},{32,48},{1,17},{17,33},{33,49},{2,18},{18,34},{34,5... | collective-permute-start | bytes 36872
Sparse Core Ops, SparseCore 0:
  10.1 115.7 all-gather.3
  128.6 52.0 all-gather.5
  183.5 62.8 reduce-scatter.3
